TPU v7x, 256 devices: a whole 4x4x8 slice. The times are simulated.
256 devices in a mesh: win: 32 (over y, x, core), grp: 8 (over z).
Axes of the slice: x: 4, y: 4, z: 8, core: 2. Of those that a mesh axis runs over, the one named last changes fastest.
Arguments:
- traces: bfloat16 [256, 512, 2048], P(('win', 'grp'))
- pair_lists: int32 [32, 3], P('win'), may hold values from -1 to 3, as said below
- observed: float32 [32, 3, 16, 16, 2048], P('win'), may hold values from -4 to 4
Outputs:
- correl: float32 [32, 3, 16, 16, 2048], P('win', None, None, None, 'grp')
- trace_gradient: bfloat16 [256, 512, 2048], P(('win', 'grp'))
Inputs may be any that keep to these rules, and one draw needn't show every extreme that they name: `pair_lists`: each row lists distinct offsets in increasing order, followed by -1 in its empty slots; block a lists only offsets o with a + o < 32; every block lists at least one offset, and block 0 fills all 3 slots and lists offset 4 - 1.
All inputs are finite; a program needn't handle non-finite values.
Results may differ from a plain program's by a relative error of at most 0.014.
Values may be sent and summed in bfloat16 or wider, within the bound.
No kernel may reach another device: no remote copies, remote signals or barrier semaphores. Data moves between devices by JAX's collectives and lax.ppermute only.
A program may use at most 192 MiB of HBM per device.

v0:
```python
import math
import jax
import jax.numpy as jnp
from jax import lax
from jax.sharding import PartitionSpec as P

SEG = 2048
FREQ = 1024
BAND = 64
OFFSETS = 4


def passed_along(array, axis, by):
    peers = lax.axis_size(axis)
    pairs = [(i, i + by) for i in range(peers) if 0 <= i + by < peers]
    return lax.ppermute(array, axis, pairs)


def dft_table(first_column, column_count):
    samples = jnp.arange(SEG, dtype=jnp.int32)
    columns = first_column + jnp.arange(column_count, dtype=jnp.int32)
    harmonic = columns % FREQ
    phases = samples[:, None] * harmonic[None, :] % SEG
    angles = phases.astype(jnp.float32) * (2.0 * math.pi / SEG)
    values = jnp.where(columns[None, :] < FREQ, jnp.cos(angles), -jnp.sin(angles))
    return values.astype(jnp.bfloat16)


def whiten(spectrum):
    halfway = spectrum.shape[-1] // 2
    real_part = spectrum[..., :halfway]
    imag_part = spectrum[..., halfway:]
    power_bins = real_part * real_part + imag_part * imag_part
    banded = power_bins.reshape(power_bins.shape[:-1] + (halfway // BAND, BAND))
    inverse = lax.rsqrt(jnp.mean(banded, axis=-1) + 1e-05)
    spread = jnp.broadcast_to(inverse[..., None], banded.shape).reshape(power_bins.shape)
    return spectrum * jnp.concatenate([spread, spread], axis=-1)


def split_halves(operand):
    halfway = operand.shape[-1] // 2
    return (operand[..., :halfway], operand[..., halfway:])


def widen(operand):
    return operand.astype(jnp.float32)


def correlate(leading, trailing, windows_total):
    lead_real, lead_imag = split_halves(leading)
    trail_real, trail_imag = split_halves(trailing)
    left_real = widen(lead_real)[:, :, None, :]
    left_imag = widen(lead_imag)[:, :, None, :]
    right_real = widen(trail_real)[:, None, :, :]
    right_imag = widen(trail_imag)[:, None, :, :]
    real_sum = jnp.sum(left_real * right_real + left_imag * right_imag, axis=0)
    imag_sum = jnp.sum(left_real * right_imag - left_imag * right_real, axis=0)
    return jnp.concatenate([real_sum, imag_sum], axis=-1) / windows_total


def pull_first(residual, trailing):
    resid_real, resid_imag = split_halves(residual)
    trail_real, trail_imag = split_halves(trailing)
    left_real = widen(resid_real)[None]
    left_imag = widen(resid_imag)[None]
    right_real = widen(trail_real)[:, None, :, :]
    right_imag = widen(trail_imag)[:, None, :, :]
    real_part = jnp.sum(left_real * right_real + left_imag * right_imag, axis=2)
    imag_part = jnp.sum(left_real * right_imag - left_imag * right_real, axis=2)
    return jnp.concatenate([real_part, imag_part], axis=-1)


def pull_second(residual, leading):
    resid_real, resid_imag = split_halves(residual)
    lead_real, lead_imag = split_halves(leading)
    left_real = widen(resid_real)[None]
    left_imag = widen(resid_imag)[None]
    right_real = widen(lead_real)[:, :, None, :]
    right_imag = widen(lead_imag)[:, :, None, :]
    real_part = jnp.sum(left_real * right_real - left_imag * right_imag, axis=1)
    imag_part = jnp.sum(left_real * right_imag + left_imag * right_real, axis=1)
    return jnp.concatenate([real_part, imag_part], axis=-1)


def on_device(traces, pair_lists, observed):
    win_dev, channels, samples = traces.shape
    column_total = 2 * FREQ
    column_step = min(512, column_total)
    tables = [
        dft_table(start_col, column_step) for start_col in range(0, column_total, column_step)
    ]
    flat_traces = traces.reshape(win_dev * channels, samples)
    spectra = jnp.concatenate(
        [
            jnp.dot(flat_traces, table_part, preferred_element_type=jnp.float32)
            for table_part in tables
        ],
        axis=1,
    )
    spectra = spectra.reshape(win_dev, channels, column_total)
    whitened = whiten(spectra).astype(jnp.bfloat16)
    grp_count = lax.axis_size("grp")
    share_width = column_total // grp_count
    moved_blocks = lax.all_to_all(whitened, "win", split_axis=1, concat_axis=0, tiled=True)
    windows_total = moved_blocks.shape[0] * grp_count
    partner_list = [moved_blocks] + [
        passed_along(moved_blocks, "win", -offset) for offset in range(1, OFFSETS)
    ]
    stacked = jnp.stack(partner_list)
    offsets = pair_lists[0]
    slot_total = offsets.shape[0]
    live_slots = (offsets >= 0).astype(jnp.float32)[:, None, None, None]
    partners = [
        lax.dynamic_index_in_dim(stacked, jnp.maximum(offsets[slot_index], 0), 0, keepdims=False)
        for slot_index in range(slot_total)
    ]
    correl = (
        jnp.stack(
            [correlate(moved_blocks, partner_block, windows_total) for partner_block in partners]
        )
        * live_slots
    )
    share_start = lax.axis_index("grp") * share_width
    totals = lax.psum(correl, "grp")
    correl_share = lax.dynamic_slice_in_dim(totals, share_start, share_width, 3)
    residual = ((totals - observed[0]) * live_slots).astype(jnp.bfloat16)
    own_grad = pull_first(residual[0], partners[0])
    for slot_index in range(1, slot_total):
        own_grad = own_grad + pull_first(residual[slot_index], partners[slot_index])
    contrib = []
    for offset in range(OFFSETS):
        chosen = jnp.zeros_like(residual[0])
        for slot_index in range(slot_total):
            chosen = jnp.where(offsets[slot_index] == offset, residual[slot_index], chosen)
        contrib.append(pull_second(chosen, moved_blocks))
    white_grad = own_grad + contrib[0]
    for offset in range(1, OFFSETS):
        white_grad = white_grad + passed_along(
            contrib[offset].astype(jnp.bfloat16), "win", offset
        ).astype(jnp.float32)
    returned = lax.all_to_all(
        white_grad.astype(jnp.bfloat16), "win", split_axis=0, concat_axis=1, tiled=True
    )
    unused, pullback = jax.vjp(whiten, spectra)
    spectra_grad = pullback(returned.astype(jnp.float32))[0].astype(jnp.bfloat16)
    flat_grad = spectra_grad.reshape(win_dev * channels, column_total)
    trace_grad = jnp.zeros((win_dev * channels, samples), jnp.float32)
    for table_index in range(len(tables)):
        start_col = table_index * column_step
        trace_grad = trace_grad + jnp.dot(
            flat_grad[:, start_col : start_col + column_step],
            tables[table_index].T,
            preferred_element_type=jnp.float32,
        )
    return (correl_share[None], trace_grad.reshape(win_dev, channels, samples).astype(jnp.bfloat16))


def solution(mesh):
    return jax.shard_map(
        on_device,
        mesh=mesh,
        in_specs=(P(("win", "grp"), None, None), P("win", None), P("win", None, None, None, None)),
        out_specs=(P("win", None, None, None, "grp"), P(("win", "grp"), None, None)),
        check_vma=False,
    )
```

profile of v0, /device:TPU:1, one launch (start us, length us, event | category | flops | bytes accessed | tf_op | source)
XLA Modules:
  0.0 817.0 jit_solution(5095351248463171921)
XLA Ops:
  8.8 17.5 %fusion.41 = f32[512,512]{1,0:T(8,128)S(1)} fusion(bf16[1,512,2048]{2,1,0:T(8,128)(2,1)S(1)} %copy-done, s32[512]{0:T(512)S(1)} %add_select_fusion.4, pred[512]{0:T(512)(128)(4,1)S(1)} %fusion.60), kind=kOutput, calls=%fused_computation.95 | convolution fusion | flops 1091567616 | bytes 3148288 | tf_op jit(solution)/shard_map/dot_general | solution.py:95
  26.2 17.2 %fusion.43 = f32[512,512]{1,0:T(8,128)S(1)} fusion(bf16[1,512,2048]{2,1,0:T(8,128)(2,1)S(1)} %copy-done, s32[512]{0:T(512)S(1)} %add_select_fusion.5, pred[512]{0:T(512)(128)(4,1)S(1)} %fusion.61), kind=kOutput, calls=%fused_computation.97 | convolution fusion | flops 1091567616 | bytes 3148288 | tf_op jit(solution)/shard_map/dot_general | solution.py:95
  43.4 17.6 %fusion.45 = f32[512,512]{1,0:T(8,128)S(1)} fusion(bf16[1,512,2048]{2,1,0:T(8,128)(2,1)S(1)} %copy-done, s32[512]{0:T(512)S(1)} %add_select_fusion.6, pred[512]{0:T(512)(128)(4,1)S(1)} %fusion.62), kind=kOutput, calls=%fused_computation.99 | convolution fusion | flops 1091567616 | bytes 3148288 | tf_op jit(solution)/shard_map/dot_general | solution.py:95
  61.0 17.2 %fusion.47 = f32[512,512]{1,0:T(8,128)S(1)} fusion(bf16[1,512,2048]{2,1,0:T(8,128)(2,1)S(1)} %copy-done, s32[512]{0:T(512)S(1)} %add_select_fusion.7, pred[512]{0:T(512)(128)(4,1)S(1)} %iota_compare_fusion), kind=kOutput, calls=%fused_computation.101 | convolution fusion | flops 1091567616 | bytes 3148288 | tf_op jit(solution)/shard_map/dot_general | solution.py:95
  82.7 3.9 fusion.16
  86.6 10.8 %copy.14 = bf16[1,512,2048]{2,0,1:T(2,128)(2,1)} copy(bf16[1,512,2048]{1,2,0:T(8,128)(2,1)} %fusion.16) | data formatting | bytes 4194304 | tf_op jit(solution)/shard_map/convert_element_type | solution.py:101
  98.0 13.2 %reduce.2 = bf16[512,2048]{1,0:T(8,128)(2,1)S(1)} reduce(bf16[512,1,2048]{2,1,0:T(2,128)(2,1)} %bitcast.118, bf16[]{:T(256)} %broadcast.306), dimensions={1}, to_apply=%bitcast.108.reduce_sub_computation | reduce | bytes 4194306
  113.9 37.0 %all_to_all.21 = bf16[32,2,16384]{2,1,0:T(2,128)(2,1)S(1)} all-to-all(bf16[32,2,16384]{2,1,0:T(2,128)(2,1)} %reshape.499), channel_id=1, replica_groups=mesh['win'=32,'grp'=8] {'win'}, dimensions={0} | all-to-all | bytes 4194304 | tf_op jit(solution)/shard_map/all_to_all | solution.py:104
  150.9 6.8 reshape.500
  157.6 3.5 copy.17
  171.1 18.9 %collective-permute-done.2 = bf16[32,16,2048]{2,1,0:T(8,128)(2,1)S(1)} collective-permute-done((bf16[32,16,2048]{2,1,0:T(8,128)(2,1)S(1)}, bf16[32,16,2048]{2,1,0:T(8,128)(2,1)S(1)}, u32[]{:S(2)}, u32[]{:S(2)}) %collective-permute-start.2) | collective-permute-done | bytes 2097184 | tf_op jit(solution)/shard_map/ppermute | solution.py:16
  190.0 63.7 %collective-permute-done.1 = bf16[32,16,2048]{2,1,0:T(8,128)(2,1)S(1)} collective-permute-done((bf16[32,16,2048]{2,1,0:T(8,128)(2,1)S(1)}, bf16[32,16,2048]{2,1,0:T(8,128)(2,1)S(1)}, u32[]{:S(2)}, u32[]{:S(2)}) %collective-permute-start.1) | collective-permute-done | bytes 2097184 | tf_op jit(solution)/shard_map/ppermute | solution.py:16
  259.6 3.7 slice_convert_fusion
  263.3 35.8 %add_reduce_fusion.9 = (f32[16,16,1024]{2,1,0:T(8,128)}, f32[16,16,1024]{2,1,0:T(8,128)}, f32[16,16,1024]{2,1,0:T(8,128)}, f32[16,16,1024]{2,1,0:T(8,128)}, f32[16,16,1024]{2,1,0:T(8,128)}, /*index=5*/f32[16,16,1024]{2,1,0:T(8,128)}) fusion(f32[32,16,1024]{2,1,0:T(8,128)} %get-tuple-element.50, f32[32,16,1024]{2,1,0:T(8,128)} %get-tuple-element.48, ...), kind=kLoop, calls=%fused_computation.19 | loop fusion | flops 199753728 | bytes 23068672 | tf_op jit(solution)/shard_map/reduce_sum | solution.py:56
  313.0 164.2 %all-reduce.4.cloned.1.call-done = f32[3,16,16,2048]{3,2,1,0:T(8,128)} async-done(((f32[3,16,16,2048]{3,2,1,0:T(8,128)}), f32[3,16,16,2048]{3,2,1,0:T(8,128)}) %all-reduce.4.cloned.1.call-update) | async-done | bytes 6291472 | tf_op jit(solution)/shard_map/psum | solution.py:124
  477.2 6.4 fusion.1
  488.2 70.5 %subtract_reduce_fusion.2 = (bf16[32,16,1024]{2,1,0:T(8,128)(2,1)S(1)}, bf16[32,16,1024]{2,1,0:T(8,128)(2,1)S(1)}, f32[32,16,1024]{2,1,0:T(8,128)S(1)}, f32[32,1...) fusion(f32[16,16,1024]{2,1,0:T(8,128)S(1)} %get-tuple-element.5, ...), kind=kLoop, calls=%fused_computation.5 | loop fusion | flops 264241152 | bytes 23068672 | tf_op jit(solution)/shard_map/reduce_sum | solution.py:80
  560.6 6.5 collective-permute-start.5
  573.7 20.6 %add_reduce_fusion.4 = (f32[32,16,1024]{2,1,0:T(8,128)S(1)}, f32[32,16,1024]{2,1,0:T(8,128)S(1)}) fusion(f32[16,16,1024]{2,1,0:T(8,128)S(1)} %get-tuple-element.60, f32[16,16,1024]{2,1,0:T(8,128)S(1)} %get-tuple-element.59, f32[32,16,1024]{2,1,0:T(8,128)S(1)} %copy-done.9, f32[32,16,1024]{2,1,0:T(8,128)S(1)} %copy-done.10), kind=kLoop, calls=%fused_computation.9 | loop fusion | flops 66060288 | bytes 10485760 | tf_op jit(solution)/shard_map/reduce_sum | solution.py:68
  594.3 20.6 %add_reduce_fusion.5 = (f32[32,16,1024]{2,1,0:T(8,128)S(1)}, f32[32,16,1024]{2,1,0:T(8,128)S(1)}) fusion(f32[16,16,1024]{2,1,0:T(8,128)S(1)} %get-tuple-element.62, f32[16,16,1024]{2,1,0:T(8,128)S(1)} %get-tuple-element.61, f32[32,16,1024]{2,1,0:T(8,128)S(1)} %copy-done.8, f32[32,16,1024]{2,1,0:T(8,128)S(1)} %copy-done.7), kind=kLoop, calls=%fused_computation.11 | loop fusion | flops 66060288 | bytes 10485760 | tf_op jit(solution)/shard_map/reduce_sum | solution.py:68
  616.5 20.5 %add_reduce_fusion.6 = (f32[32,16,1024]{2,1,0:T(8,128)S(1)}, f32[32,16,1024]{2,1,0:T(8,128)S(1)}) fusion(f32[16,16,1024]{2,1,0:T(8,128)S(1)} %get-tuple-element.64, f32[16,16,1024]{2,1,0:T(8,128)S(1)} %get-tuple-element.63, f32[32,16,1024]{2,1,0:T(8,128)S(1)} %copy-done.4, f32[32,16,1024]{2,1,0:T(8,128)S(1)} %get-tuple-element.49), kind=kLoop, calls=%fused_computation.13 | loop fusion | flops 66060288 | bytes 10485760 | tf_op jit(solution)/shard_map/reduce_sum | solution.py:68
  637.1 17.6 %collective-permute-done.4 = bf16[32,16,2048]{2,1,0:T(8,128)(2,1)} collective-permute-done((bf16[32,16,2048]{2,1,0:T(8,128)(2,1)S(1)}, bf16[32,16,2048]{2,1,0:T(8,128)(2,1)}, u32[]{:S(2)}, u32[]{:S(2)}) %collective-permute-start.4) | collective-permute-done | bytes 2097184 | tf_op jit(solution)/shard_map/ppermute | solution.py:16
  654.6 22.6 %collective-permute-done.3 = bf16[32,16,2048]{2,1,0:T(8,128)(2,1)} collective-permute-done((bf16[32,16,2048]{2,1,0:T(8,128)(2,1)}, bf16[32,16,2048]{2,1,0:T(8,128)(2,1)}, u32[]{:S(2)}, u32[]{:S(2)}) %collective-permute-start.3) | collective-permute-done | bytes 2097184 | tf_op jit(solution)/shard_map/ppermute | solution.py:16
  677.2 5.7 fusion.25
  682.9 8.8 %all-to-all-start.1 = ((bf16[32,16,2048]{2,1,0:T(8,128)(2,1)}), bf16[32,16,2048]{2,1,0:T(8,128)(2,1)S(1)}, u32[]{:S(2)}, u32[]{:S(2)}) async-start(bf16[32,16,2048]{2,1,0:T(8,128)(2,1)} %fusion.25), calls=%async_computation.1 | async-start | bytes 4194304 | tf_op jit(solution)/shard_map/all_to_all | solution.py:141
  693.8 25.7 %all-to-all-done.1 = bf16[32,16,2048]{2,1,0:T(8,128)(2,1)S(1)} async-done(((bf16[32,16,2048]{2,1,0:T(8,128)(2,1)}), bf16[32,16,2048]{2,1,0:T(8,128)(2,1)S(1)}, u32[]{:S(2)}, u32[]{:S(2)}) %all-to-all-start.1) | async-done | bytes 2097184 | tf_op jit(solution)/shard_map/all_to_all | solution.py:141
  721.9 5.5 copy.15
  727.4 3.5 fusion.39
  737.3 17.7 %fusion.49 = f32[512,2048]{1,0:T(8,128)S(1)} fusion(s32[512]{0:T(512)S(1)} %add_select_fusion.5, pred[512]{0:T(512)(128)(4,1)S(1)} %fusion.61, bf16[512,2048]{0,1:T(8,128)(2,1)S(1)} %fusion.40), kind=kOutput, calls=%fused_computation.107 | convolution fusion | flops 1091567616 | bytes 4721152 | tf_op jit(solution)/shard_map/dot_general | solution.py:150
  755.0 17.8 %fusion.50 = f32[512,2048]{1,0:T(8,128)S(1)} fusion(s32[512]{0:T(512)S(1)} %add_select_fusion.6, pred[512]{0:T(512)(128)(4,1)S(1)} %fusion.62, bf16[512,2048]{0,1:T(8,128)(2,1)S(1)} %fusion.40), kind=kOutput, calls=%fused_computation.108 | convolution fusion | flops 1091567616 | bytes 4721152 | tf_op jit(solution)/shard_map/dot_general | solution.py:150
  772.8 18.1 %fusion.51 = f32[512,2048]{1,0:T(8,128)S(1)} fusion(s32[512]{0:T(512)S(1)} %add_select_fusion.7, pred[512]{0:T(512)(128)(4,1)S(1)} %iota_compare_fusion, bf16[512,2048]{0,1:T(8,128)(2,1)S(1)} %fusion.40), kind=kOutput, calls=%fused_computation.109 | convolution fusion | flops 1091567616 | bytes 4721152 | tf_op jit(solution)/shard_map/dot_general | solution.py:150
  791.0 19.0 %fusion.38 = bf16[1,512,2048]{2,1,0:T(8,128)(2,1)} fusion(f32[512,2048]{1,0:T(8,128)S(1)} %fusion.49, f32[512,2048]{1,0:T(8,128)S(1)} %fusion.51, f32[512,2048]{1,0:T(8,128)S(1)} %fusion.50, s32[512]{0:T(512)S(1)} %add_select_fusion.4, pred[512]{0:T(512)(128)(4,1)S(1)} %fusion.60, bf16[512,2048]{0,1:T(8,128)(2,1)S(1)} %fusion.40), kind=kOutput, calls=%fused_computation.84 | convolution fusion | flops 1095761920 | bytes 15206912 | tf_op jit(solution)/shard_map/dot_general | solution.py:150
  (106 shorter events, 55.0 us)
Async XLA Ops:
  7.2 1.6 copy-start
  7.2 470.0 %all-reduce.4.cloned.1.call-start = ((), (), s32[]{:S(2)}) async-start(), calls=%async_computation.2 | async-start | bytes 12582912 | tf_op jit(solution)/shard_map/psum | solution.py:124
  43.4 34.8 %copy-start.13 = (f32[512,512]{1,0:T(8,128)}, f32[512,512]{1,0:T(8,128)S(1)}, u32[]{:S(2)}) copy-start(f32[512,512]{1,0:T(8,128)S(1)} %fusion.43) | copy-start | bytes 3145732
  61.0 17.2 %copy-start.15 = (f32[512,512]{1,0:T(8,128)}, f32[512,512]{1,0:T(8,128)S(1)}, u32[]{:S(2)}) copy-start(f32[512,512]{1,0:T(8,128)S(1)} %fusion.45) | copy-start | bytes 3145732
  79.2 2.0 copy-start.3
  82.6 3.9 copy-start.5
  157.6 8.4 %copy-start.25 = (s32[1,3]{1,0:T(1,128)S(1)}, s32[1,3]{1,0:T(1,128)}, u32[]{:S(2)}) copy-start(s32[1,3]{1,0:T(1,128)} %param.4) | copy-start | bytes 40
  161.1 28.9 %collective-permute-start.2 = (bf16[32,16,2048]{2,1,0:T(8,128)(2,1)S(1)}, bf16[32,16,2048]{2,1,0:T(8,128)(2,1)S(1)}, u32[]{:S(2)}, u32[]{:S(2)}) collective-permute-start(bf16[32,16,2048]{2,1,0:T(8,128)(2,1)S(1)} %bitcast.111), channel_id=1, source_target_pairs={{24,0},{32,8},{40,16},{48,24},{56,32},{64,40},{72,48},{80,56},{88,... | collective-permute-start | bytes 6291464 | tf_op jit(solution)/shard_map/ppermute | solution.py:16
  162.4 91.2 %collective-permute-start.1 = (bf16[32,16,2048]{2,1,0:T(8,128)(2,1)S(1)}, bf16[32,16,2048]{2,1,0:T(8,128)(2,1)S(1)}, u32[]{:S(2)}, u32[]{:S(2)}) collective-permute-start(bf16[32,16,2048]{2,1,0:T(8,128)(2,1)S(1)} %bitcast.112), channel_id=1, source_target_pairs={{16,0},{24,8},{32,16},{40,24},{48,32},{56,40},{64,48},{72,56},{80,... | collective-permute-start | bytes 6291464 | tf_op jit(solution)/shard_map/ppermute | solution.py:16
  163.7 91.9 %collective-permute-start = (bf16[32,16,2048]{2,1,0:T(8,128)(2,1)S(1)}, bf16[32,16,2048]{2,1,0:T(8,128)(2,1)S(1)}, u32[]{:S(2)}, u32[]{:S(2)}) collective-permute-start(bf16[32,16,2048]{2,1,0:T(8,128)(2,1)S(1)} %bitcast.113), channel_id=1, source_target_pairs={{8,0},{16,8},{24,16},{32,24},{40,32},{48,40},{56,48},{64,56},{72,6... | collective-permute-start | bytes 6291464 | tf_op jit(solution)/shard_map/ppermute | solution.py:16
  299.1 1.9 copy-start.23
  299.1 2.2 copy-start.24
  299.1 2.5 copy-start.21
  299.1 2.8 copy-start.22
  486.0 2.2 copy-start.12
  558.7 8.4 %copy-start.19 = (bf16[32,16,1024]{2,1,0:T(8,128)(2,1)S(1)}, bf16[32,16,1024]{2,1,0:T(8,128)(2,1)}, u32[]{:S(2)}) copy-start(bf16[32,16,1024]{2,1,0:T(8,128)(2,1)} %get-tuple-element.24) | copy-start | bytes 3145732
  558.7 8.4 %copy-start.20 = (bf16[32,16,1024]{2,1,0:T(8,128)(2,1)S(1)}, bf16[32,16,1024]{2,1,0:T(8,128)(2,1)}, u32[]{:S(2)}) copy-start(bf16[32,16,1024]{2,1,0:T(8,128)(2,1)} %get-tuple-element.25) | copy-start | bytes 3145732
  560.6 76.5 %collective-permute-start.5 = (bf16[32,16,2048]{2,1,0:T(8,128)(2,1)S(1)}, bf16[32,16,2048]{2,1,0:T(8,128)(2,1)}, u32[]{:S(2)}, u32[]{:S(2)}) collective-permute-start(bf16[32,16,2048]{2,1,0:T(8,128)(2,1)S(1)} %pad_maximum_fusion.5), channel_id=1, source_target_pairs={{0,24},{8,32},{16,40},{24,48},{32,56},{40,64},{48,72},{56,80},{64,... | collective-permute-start | bytes 6291464 | tf_op jit(solution)/shard_map/ppermute | solution.py:16
  567.1 6.6 copy-start.9
  567.1 6.6 copy-start.10
  567.3 87.3 %collective-permute-start.4 = (bf16[32,16,2048]{2,1,0:T(8,128)(2,1)S(1)}, bf16[32,16,2048]{2,1,0:T(8,128)(2,1)}, u32[]{:S(2)}, u32[]{:S(2)}) collective-permute-start(bf16[32,16,2048]{2,1,0:T(8,128)(2,1)S(1)} %pad_maximum_fusion.4), channel_id=1, source_target_pairs={{0,16},{8,24},{16,32},{24,40},{32,48},{40,56},{48,64},{56,72},{64,... | collective-permute-start | bytes 6291464 | tf_op jit(solution)/shard_map/ppermute | solution.py:16
  571.7 105.5 %collective-permute-start.3 = (bf16[32,16,2048]{2,1,0:T(8,128)(2,1)}, bf16[32,16,2048]{2,1,0:T(8,128)(2,1)}, u32[]{:S(2)}, u32[]{:S(2)}) collective-permute-start(bf16[32,16,2048]{2,1,0:T(8,128)(2,1)} %pad_maximum_fusion.3), channel_id=1, source_target_pairs={{0,8},{8,16},{16,24},{24,32},{32,40},{40,48},{48,56},{56,64},{64,7... | collective-permute-start | bytes 6291464 | tf_op jit(solution)/shard_map/ppermute | solution.py:16
  573.7 20.6 %copy-start.7 = (f32[32,16,1024]{2,1,0:T(8,128)S(1)}, f32[32,16,1024]{2,1,0:T(8,128)}, u32[]{:S(2)}) copy-start(f32[32,16,1024]{2,1,0:T(8,128)} %get-tuple-element.68) | copy-start | bytes 6291460
  573.7 20.6 %copy-start.8 = (f32[32,16,1024]{2,1,0:T(8,128)S(1)}, f32[32,16,1024]{2,1,0:T(8,128)}, u32[]{:S(2)}) copy-start(f32[32,16,1024]{2,1,0:T(8,128)} %get-tuple-element.69) | copy-start | bytes 6291460
  594.3 20.6 %copy-start.18 = (bf16[16,16,2048]{2,1,0:T(8,128)(2,1)S(1)}, bf16[16,16,2048]{2,1,0:T(8,128)(2,1)}, u32[]{:S(2)}) copy-start(bf16[16,16,2048]{2,1,0:T(8,128)(2,1)} %get-tuple-element.42) | copy-start | bytes 3145732
  614.9 1.6 copy-start.4
  682.9 36.5 %all-to-all-start.1 = ((bf16[32,16,2048]{2,1,0:T(8,128)(2,1)}), bf16[32,16,2048]{2,1,0:T(8,128)(2,1)S(1)}, u32[]{:S(2)}, u32[]{:S(2)}) async-start(bf16[32,16,2048]{2,1,0:T(8,128)(2,1)} %fusion.25), calls=%async_computation.1 | async-start | bytes 4194304 | tf_op jit(solution)/shard_map/all_to_all | solution.py:141
  721.9 5.5 copy-start.14
  721.9 5.5 copy-start.16
  731.7 3.5 copy-start.2
  731.8 4.1 copy-start.6
  790.9 19.0 %copy-start.1 = (bf16[1,512,2048]{2,1,0:T(8,128)(2,1)S(1)}, bf16[1,512,2048]{2,1,0:T(8,128)(2,1)}, u32[]{:S(2)}) copy-start(bf16[1,512,2048]{2,1,0:T(8,128)(2,1)} %param.3) | copy-start | bytes 6291460
  (2 other events, 2.6 us)
Sparse Core Ops, SparseCore 0:
  305.7 171.4 all-reduce.3
where the time goes:
time: 826 us; the launch traced here: 817 us
  waiting for transfers between devices  315 us (38%)
  other arithmetic  230 us (28%)
  matrix products  142 us (17%)
  local copies, waits for them, and re-layouts  43.9 us (5%)
  blocking collectives  37 us (4%)
  starting transfers between devices  25.1 us (3%)
  between operations  24.1 us (3%)
    psum x1, waiting for transfers between devices, on_device(): totals = lax.psum(correl, 'grp')  164 us
    ppermute x6, waiting for transfers between devices, passed_along(): return lax.ppermute(array, axis, pairs)  125 us
    dot_general x4, matrix products, on_device(): jnp.dot(flat_grad[:, start_col:start_col + column_step], tables[table_ind...  72.6 us
    reduce_sum x1, other arithmetic, pull_second(): real_part = jnp.sum(left_real * right_real - left_imag * right_imag, axis=1)  70.5 us
    dot_general x4, matrix products, on_device(): jnp.dot(flat_traces, table_part, preferred_element_type=jnp.float32)  69.4 us
    reduce_sum x3, other arithmetic, pull_first(): real_part = jnp.sum(left_real * right_real + left_imag * right_imag, axis=2)  61.7 us
    all_to_all x1, blocking collectives, on_device(): lax.all_to_all(whitened, 'win', split_axis=1, concat_axis=0, tiled=True)  37 us
    reduce_sum x1, other arithmetic, correlate(): real_sum = jnp.sum(left_real * right_real + left_imag * right_imag, axis=0)  35.8 us
  transfers between devices with their start and end apart: 8, of which 7 were waited for; matrix products, arithmetic and copies ran while one was open for 8% of the time, Pallas kernels for 0%

commit v1 on v0

--- a/solution.py
+++ b/solution.py
@@ -101,7 +101,10 @@
     whitened = whiten(spectra).astype(jnp.bfloat16)
     grp_count = lax.axis_size("grp")
     share_width = column_total // grp_count
-    moved_blocks = lax.all_to_all(whitened, "win", split_axis=1, concat_axis=0, tiled=True)
+    moved_blocks = jnp.concatenate(
+        lax.all_to_all(jnp.stack(jnp.split(whitened, lax.axis_size("win"), axis=1)), "win", 0, 0),
+        axis=0,
+    )
     windows_total = moved_blocks.shape[0] * grp_count
     partner_list = [moved_blocks] + [
         passed_along(moved_blocks, "win", -offset) for offset in range(1, OFFSETS)

time: 826 us -> 878 us (1.063)
  local copies, waits for them, and re-layouts: 43.9 us -> 109 us
  other arithmetic: 230 us -> 215 us
    another operation x0 -> x35, local copies, waits for them, and re-layouts: none -> 55.3 us  [on_device(): jnp.stack(jnp.split(whitened, lax.axis_size('win'), axis=1))]
    unnamed x56 -> x121, local copies, waits for them, and re-layouts: 22.2 us -> 43.1 us
    unnamed x1 -> x0, other arithmetic: 13.2 us -> none
    convert_element_type x1 -> x0, local copies, waits for them, and re-layouts: 10.8 us -> none  [on_device(): whitened = whiten(spectra).astype(jnp.bfloat16)]
where the time goes in v1:
time: 878 us; the launch traced here: 867 us
  waiting for transfers between devices  314 us (36%)
  other arithmetic  215 us (24%)
  matrix products  142 us (16%)
  local copies, waits for them, and re-layouts  109 us (12%)
  blocking collectives  37 us (4%)
  starting transfers between devices  25.5 us (3%)
  between operations  24.7 us (3%)
    psum x1, waiting for transfers between devices, on_device(): totals = lax.psum(correl, 'grp')  164 us
    ppermute x6, waiting for transfers between devices, passed_along(): return lax.ppermute(array, axis, pairs)  124 us
    dot_general x4, matrix products, on_device(): jnp.dot(flat_grad[:, start_col:start_col + column_step], tables[table_ind...  72.6 us
    reduce_sum x1, other arithmetic, pull_second(): real_part = jnp.sum(left_real * right_real - left_imag * right_imag, axis=1)  70.5 us
    dot_general x4, matrix products, on_device(): jnp.dot(flat_traces, table_part, preferred_element_type=jnp.float32)  69.4 us
    reduce_sum x3, other arithmetic, pull_first(): real_part = jnp.sum(left_real * right_real + left_imag * right_imag, axis=2)  61.7 us
    another operation x35, local copies, waits for them, and re-layouts, on_device(): jnp.stack(jnp.split(whitened, lax.axis_size('win'), axis=1))  55.3 us
    unnamed x121, local copies, waits for them, and re-layouts  43.1 us
  transfers between devices with their start and end apart: 8, of which 7 were waited for; matrix products, arithmetic and copies ran while one was open for 8% of the time, Pallas kernels for 0%

profile of v1, /device:TPU:1, one launch (start us, length us, event | category | flops | bytes accessed | tf_op | source)
XLA Modules:
  0.0 867.4 jit_solution(3310101252329556649)
XLA Ops:
  8.8 17.5 %fusion.41 = f32[512,512]{1,0:T(8,128)S(1)} fusion(bf16[1,512,2048]{2,1,0:T(8,128)(2,1)S(1)} %copy-done, s32[512]{0:T(512)S(1)} %add_select_fusion.4, pred[512]{0:T(512)(128)(4,1)S(1)} %fusion.60), kind=kOutput, calls=%fused_computation.95 | convolution fusion | flops 1091567616 | bytes 3148288 | tf_op jit(solution)/shard_map/dot_general | solution.py:95
  26.2 17.2 %fusion.43 = f32[512,512]{1,0:T(8,128)S(1)} fusion(bf16[1,512,2048]{2,1,0:T(8,128)(2,1)S(1)} %copy-done, s32[512]{0:T(512)S(1)} %add_select_fusion.5, pred[512]{0:T(512)(128)(4,1)S(1)} %fusion.61), kind=kOutput, calls=%fused_computation.97 | convolution fusion | flops 1091567616 | bytes 3148288 | tf_op jit(solution)/shard_map/dot_general | solution.py:95
  43.4 17.6 %fusion.45 = f32[512,512]{1,0:T(8,128)S(1)} fusion(bf16[1,512,2048]{2,1,0:T(8,128)(2,1)S(1)} %copy-done, s32[512]{0:T(512)S(1)} %add_select_fusion.6, pred[512]{0:T(512)(128)(4,1)S(1)} %fusion.62), kind=kOutput, calls=%fused_computation.99 | convolution fusion | flops 1091567616 | bytes 3148288 | tf_op jit(solution)/shard_map/dot_general | solution.py:95
  61.0 17.2 %fusion.47 = f32[512,512]{1,0:T(8,128)S(1)} fusion(bf16[1,512,2048]{2,1,0:T(8,128)(2,1)S(1)} %copy-done, s32[512]{0:T(512)S(1)} %add_select_fusion.7, pred[512]{0:T(512)(128)(4,1)S(1)} %iota_compare_fusion), kind=kOutput, calls=%fused_computation.101 | convolution fusion | flops 1091567616 | bytes 3148288 | tf_op jit(solution)/shard_map/dot_general | solution.py:95
  86.0 4.5 slice_bitcast_fusion.22
  90.5 4.9 slice_bitcast_fusion.3
  174.5 37.0 %all_to_all.14 = bf16[32,1,16,2048]{3,2,1,0:T(8,128)(2,1)S(1)} all-to-all(bf16[32,1,16,2048]{3,2,1,0:T(8,128)(2,1)} %constant_dynamic-update-slice_fusion), channel_id=1, replica_groups=mesh['win'=32,'grp'=8] {'win'}, dimensions={0} | all-to-all | bytes 4194304 | tf_op jit(solution)/shard_map/all_to_all | solution.py:105
  222.0 18.4 %collective-permute-done.2 = bf16[32,16,2048]{2,1,0:T(8,128)(2,1)S(1)} collective-permute-done((bf16[32,16,2048]{2,1,0:T(8,128)(2,1)S(1)}, bf16[32,16,2048]{2,1,0:T(8,128)(2,1)S(1)}, u32[]{:S(2)}, u32[]{:S(2)}) %collective-permute-start.2) | collective-permute-done | bytes 2097184 | tf_op jit(solution)/shard_map/ppermute | solution.py:16
  240.4 63.7 %collective-permute-done.1 = bf16[32,16,2048]{2,1,0:T(8,128)(2,1)S(1)} collective-permute-done((bf16[32,16,2048]{2,1,0:T(8,128)(2,1)S(1)}, bf16[32,16,2048]{2,1,0:T(8,128)(2,1)S(1)}, u32[]{:S(2)}, u32[]{:S(2)}) %collective-permute-start.1) | collective-permute-done | bytes 2097184 | tf_op jit(solution)/shard_map/ppermute | solution.py:16
  310.0 3.7 slice_convert_fusion
  313.7 35.8 %add_reduce_fusion.9 = (f32[16,16,1024]{2,1,0:T(8,128)}, f32[16,16,1024]{2,1,0:T(8,128)}, f32[16,16,1024]{2,1,0:T(8,128)}, f32[16,16,1024]{2,1,0:T(8,128)}, f32[16,16,1024]{2,1,0:T(8,128)}, /*index=5*/f32[16,16,1024]{2,1,0:T(8,128)}) fusion(f32[32,16,1024]{2,1,0:T(8,128)} %get-tuple-element.50, f32[32,16,1024]{2,1,0:T(8,128)} %get-tuple-element.48, ...), kind=kLoop, calls=%fused_computation.19 | loop fusion | flops 199753728 | bytes 23068672 | tf_op jit(solution)/shard_map/reduce_sum | solution.py:56
  352.5 3.4 maximum_multiply_fusion
  363.7 163.9 %all-reduce.4.cloned.1.call-done = f32[3,16,16,2048]{3,2,1,0:T(8,128)} async-done(((f32[3,16,16,2048]{3,2,1,0:T(8,128)}), f32[3,16,16,2048]{3,2,1,0:T(8,128)}) %all-reduce.4.cloned.1.call-update) | async-done | bytes 6291472 | tf_op jit(solution)/shard_map/psum | solution.py:127
  527.6 6.4 fusion.1
  538.6 70.5 %subtract_reduce_fusion.2 = (bf16[32,16,1024]{2,1,0:T(8,128)(2,1)S(1)}, bf16[32,16,1024]{2,1,0:T(8,128)(2,1)S(1)}, f32[32,16,1024]{2,1,0:T(8,128)S(1)}, f32[32,1...) fusion(f32[16,16,1024]{2,1,0:T(8,128)S(1)} %get-tuple-element.9, ...), kind=kLoop, calls=%fused_computation.5 | loop fusion | flops 264241152 | bytes 23068672 | tf_op jit(solution)/shard_map/reduce_sum | solution.py:80
  610.9 6.5 collective-permute-start.5
  617.7 2.9 collective-permute-start.4
  624.1 20.6 %add_reduce_fusion.4 = (f32[32,16,1024]{2,1,0:T(8,128)S(1)}, f32[32,16,1024]{2,1,0:T(8,128)S(1)}) fusion(f32[16,16,1024]{2,1,0:T(8,128)S(1)} %get-tuple-element.92, f32[16,16,1024]{2,1,0:T(8,128)S(1)} %get-tuple-element.91, f32[32,16,1024]{2,1,0:T(8,128)S(1)} %copy-done.9, f32[32,16,1024]{2,1,0:T(8,128)S(1)} %copy-done.10), kind=kLoop, calls=%fused_computation.9 | loop fusion | flops 66060288 | bytes 10485760 | tf_op jit(solution)/shard_map/reduce_sum | solution.py:68
  644.7 20.6 %add_reduce_fusion.5 = (f32[32,16,1024]{2,1,0:T(8,128)S(1)}, f32[32,16,1024]{2,1,0:T(8,128)S(1)}) fusion(f32[16,16,1024]{2,1,0:T(8,128)S(1)} %get-tuple-element.94, f32[16,16,1024]{2,1,0:T(8,128)S(1)} %get-tuple-element.93, f32[32,16,1024]{2,1,0:T(8,128)S(1)} %copy-done.8, f32[32,16,1024]{2,1,0:T(8,128)S(1)} %copy-done.7), kind=kLoop, calls=%fused_computation.11 | loop fusion | flops 66060288 | bytes 10485760 | tf_op jit(solution)/shard_map/reduce_sum | solution.py:68
  666.9 20.5 %add_reduce_fusion.6 = (f32[32,16,1024]{2,1,0:T(8,128)S(1)}, f32[32,16,1024]{2,1,0:T(8,128)S(1)}) fusion(f32[16,16,1024]{2,1,0:T(8,128)S(1)} %get-tuple-element.96, f32[16,16,1024]{2,1,0:T(8,128)S(1)} %get-tuple-element.95, f32[32,16,1024]{2,1,0:T(8,128)S(1)} %copy-done.4, f32[32,16,1024]{2,1,0:T(8,128)S(1)} %get-tuple-element.49), kind=kLoop, calls=%fused_computation.13 | loop fusion | flops 66060288 | bytes 10485760 | tf_op jit(solution)/shard_map/reduce_sum | solution.py:68
  687.5 17.5 %collective-permute-done.4 = bf16[32,16,2048]{2,1,0:T(8,128)(2,1)} collective-permute-done((bf16[32,16,2048]{2,1,0:T(8,128)(2,1)S(1)}, bf16[32,16,2048]{2,1,0:T(8,128)(2,1)}, u32[]{:S(2)}, u32[]{:S(2)}) %collective-permute-start.4) | collective-permute-done | bytes 2097184 | tf_op jit(solution)/shard_map/ppermute | solution.py:16
  705.0 22.6 %collective-permute-done.3 = bf16[32,16,2048]{2,1,0:T(8,128)(2,1)} collective-permute-done((bf16[32,16,2048]{2,1,0:T(8,128)(2,1)}, bf16[32,16,2048]{2,1,0:T(8,128)(2,1)}, u32[]{:S(2)}, u32[]{:S(2)}) %collective-permute-start.3) | collective-permute-done | bytes 2097184 | tf_op jit(solution)/shard_map/ppermute | solution.py:16
  727.6 5.7 fusion.25
  733.3 8.8 %all-to-all-start.1 = ((bf16[32,16,2048]{2,1,0:T(8,128)(2,1)}), bf16[32,16,2048]{2,1,0:T(8,128)(2,1)S(1)}, u32[]{:S(2)}, u32[]{:S(2)}) async-start(bf16[32,16,2048]{2,1,0:T(8,128)(2,1)} %fusion.25), calls=%async_computation.1 | async-start | bytes 4194304 | tf_op jit(solution)/shard_map/all_to_all | solution.py:144
  744.1 25.7 %all-to-all-done.1 = bf16[32,16,2048]{2,1,0:T(8,128)(2,1)S(1)} async-done(((bf16[32,16,2048]{2,1,0:T(8,128)(2,1)}), bf16[32,16,2048]{2,1,0:T(8,128)(2,1)S(1)}, u32[]{:S(2)}, u32[]{:S(2)}) %all-to-all-start.1) | async-done | bytes 2097184 | tf_op jit(solution)/shard_map/all_to_all | solution.py:144
  772.3 5.5 copy.80
  777.8 3.5 fusion.39
  782.2 2.9 bitcast_multiply_fusion.1
  787.7 17.7 %fusion.49 = f32[512,2048]{1,0:T(8,128)S(1)} fusion(s32[512]{0:T(512)S(1)} %add_select_fusion.5, pred[512]{0:T(512)(128)(4,1)S(1)} %fusion.61, bf16[512,2048]{0,1:T(8,128)(2,1)S(1)} %fusion.40), kind=kOutput, calls=%fused_computation.107 | convolution fusion | flops 1091567616 | bytes 4721152 | tf_op jit(solution)/shard_map/dot_general | solution.py:153
  805.4 17.8 %fusion.50 = f32[512,2048]{1,0:T(8,128)S(1)} fusion(s32[512]{0:T(512)S(1)} %add_select_fusion.6, pred[512]{0:T(512)(128)(4,1)S(1)} %fusion.62, bf16[512,2048]{0,1:T(8,128)(2,1)S(1)} %fusion.40), kind=kOutput, calls=%fused_computation.108 | convolution fusion | flops 1091567616 | bytes 4721152 | tf_op jit(solution)/shard_map/dot_general | solution.py:153
  823.2 18.1 %fusion.51 = f32[512,2048]{1,0:T(8,128)S(1)} fusion(s32[512]{0:T(512)S(1)} %add_select_fusion.7, pred[512]{0:T(512)(128)(4,1)S(1)} %iota_compare_fusion, bf16[512,2048]{0,1:T(8,128)(2,1)S(1)} %fusion.40), kind=kOutput, calls=%fused_computation.109 | convolution fusion | flops 1091567616 | bytes 4721152 | tf_op jit(solution)/shard_map/dot_general | solution.py:153
  841.4 19.0 %fusion.38 = bf16[1,512,2048]{2,1,0:T(8,128)(2,1)} fusion(f32[512,2048]{1,0:T(8,128)S(1)} %fusion.49, f32[512,2048]{1,0:T(8,128)S(1)} %fusion.51, f32[512,2048]{1,0:T(8,128)S(1)} %fusion.50, s32[512]{0:T(512)S(1)} %copy-done.42, pred[512]{0:T(512)(128)(4,1)S(1)} %copy-done.44, bf16[512,2048]{0,1:T(8,128)(2,1)S(1)} %fusion.40), kind=kOutput, calls=%fused_computation.84 | convolution fusion | flops 1095761920 | bytes 15206912 | tf_op jit(solution)/shard_map/dot_general | solution.py:153
  (204 shorter events, 125.2 us)
Async XLA Ops:
  7.2 520.4 %all-reduce.4.cloned.1.call-start = ((), (), s32[]{:S(2)}) async-start(), calls=%async_computation.2 | async-start | bytes 12582912 | tf_op jit(solution)/shard_map/psum | solution.py:127
  7.3 19.0 %copy-start.43 = (pred[512]{0:T(512)(128)(4,1)}, pred[512]{0:T(512)(128)(4,1)S(1)}, u32[]{:S(2)}) copy-start(pred[512]{0:T(512)(128)(4,1)S(1)} %fusion.60) | copy-start | bytes 1540
  43.4 34.8 %copy-start.13 = (f32[512,512]{1,0:T(8,128)}, f32[512,512]{1,0:T(8,128)S(1)}, u32[]{:S(2)}) copy-start(f32[512,512]{1,0:T(8,128)S(1)} %fusion.43) | copy-start | bytes 3145732
  95.4 24.2 %copy-start.32 = (bf16[1,1,16,2048]{2,3,1,0:T(8,128)(2,1)S(1)}, bf16[1,1,16,2048]{2,3,1,0:T(8,128)(2,1)}, u32[]{:S(2)}) copy-start(bf16[1,1,16,2048]{2,3,1,0:T(8,128)(2,1)} %get-tuple-element.51) | copy-start | bytes 196612
  95.4 24.3 %copy-start.31 = (bf16[1,1,16,2048]{2,3,1,0:T(8,128)(2,1)S(1)}, bf16[1,1,16,2048]{2,3,1,0:T(8,128)(2,1)}, u32[]{:S(2)}) copy-start(bf16[1,1,16,2048]{2,3,1,0:T(8,128)(2,1)} %get-tuple-element.52) | copy-start | bytes 196612
  97.3 22.6 %copy-start.30 = (bf16[1,1,16,2048]{2,3,1,0:T(8,128)(2,1)S(1)}, bf16[1,1,16,2048]{2,3,1,0:T(8,128)(2,1)}, u32[]{:S(2)}) copy-start(bf16[1,1,16,2048]{2,3,1,0:T(8,128)(2,1)} %get-tuple-element.53) | copy-start | bytes 196612
  99.2 20.9 %copy-start.29 = (bf16[1,1,16,2048]{2,3,1,0:T(8,128)(2,1)S(1)}, bf16[1,1,16,2048]{2,3,1,0:T(8,128)(2,1)}, u32[]{:S(2)}) copy-start(bf16[1,1,16,2048]{2,3,1,0:T(8,128)(2,1)} %get-tuple-element.54) | copy-start | bytes 196612
  119.7 20.3 %copy-start.28 = (bf16[1,1,16,2048]{2,3,1,0:T(8,128)(2,1)S(1)}, bf16[1,1,16,2048]{2,3,1,0:T(8,128)(2,1)}, u32[]{:S(2)}) copy-start(bf16[1,1,16,2048]{2,3,1,0:T(8,128)(2,1)} %get-tuple-element.66) | copy-start | bytes 196612
  119.9 20.9 %copy-start.27 = (bf16[1,1,16,2048]{2,3,1,0:T(8,128)(2,1)S(1)}, bf16[1,1,16,2048]{2,3,1,0:T(8,128)(2,1)}, u32[]{:S(2)}) copy-start(bf16[1,1,16,2048]{2,3,1,0:T(8,128)(2,1)} %get-tuple-element.67) | copy-start | bytes 196612
  120.1 20.9 %copy-start.26 = (bf16[1,1,16,2048]{2,3,1,0:T(8,128)(2,1)S(1)}, bf16[1,1,16,2048]{2,3,1,0:T(8,128)(2,1)}, u32[]{:S(2)}) copy-start(bf16[1,1,16,2048]{2,3,1,0:T(8,128)(2,1)} %get-tuple-element.68) | copy-start | bytes 196612
  120.3 20.9 %copy-start.25 = (bf16[1,1,16,2048]{2,3,1,0:T(8,128)(2,1)S(1)}, bf16[1,1,16,2048]{2,3,1,0:T(8,128)(2,1)}, u32[]{:S(2)}) copy-start(bf16[1,1,16,2048]{2,3,1,0:T(8,128)(2,1)} %get-tuple-element.69) | copy-start | bytes 196612
  140.8 26.1 %copy-start.39 = (bf16[1,1,16,2048]{3,2,1,0:T(8,128)(2,1)S(1)}, bf16[1,1,16,2048]{3,2,1,0:T(8,128)(2,1)}, u32[]{:S(2)}) copy-start(bf16[1,1,16,2048]{3,2,1,0:T(8,128)(2,1)} %copy.68) | copy-start | bytes 196612
  140.8 26.7 %copy-start.38 = (bf16[1,1,16,2048]{3,2,1,0:T(8,128)(2,1)S(1)}, bf16[1,1,16,2048]{3,2,1,0:T(8,128)(2,1)}, u32[]{:S(2)}) copy-start(bf16[1,1,16,2048]{3,2,1,0:T(8,128)(2,1)} %copy.69) | copy-start | bytes 196612
  140.8 27.4 %copy-start.37 = (bf16[1,1,16,2048]{3,2,1,0:T(8,128)(2,1)S(1)}, bf16[1,1,16,2048]{3,2,1,0:T(8,128)(2,1)}, u32[]{:S(2)}) copy-start(bf16[1,1,16,2048]{3,2,1,0:T(8,128)(2,1)} %copy.70) | copy-start | bytes 196612
  140.8 28.0 %copy-start.36 = (bf16[1,1,16,2048]{3,2,1,0:T(8,128)(2,1)S(1)}, bf16[1,1,16,2048]{3,2,1,0:T(8,128)(2,1)}, u32[]{:S(2)}) copy-start(bf16[1,1,16,2048]{3,2,1,0:T(8,128)(2,1)} %copy.71) | copy-start | bytes 196612
  140.8 28.6 %copy-start.35 = (bf16[1,1,16,2048]{3,2,1,0:T(8,128)(2,1)S(1)}, bf16[1,1,16,2048]{3,2,1,0:T(8,128)(2,1)}, u32[]{:S(2)}) copy-start(bf16[1,1,16,2048]{3,2,1,0:T(8,128)(2,1)} %copy.72) | copy-start | bytes 196612
  140.8 29.3 %copy-start.34 = (bf16[1,1,16,2048]{3,2,1,0:T(8,128)(2,1)S(1)}, bf16[1,1,16,2048]{3,2,1,0:T(8,128)(2,1)}, u32[]{:S(2)}) copy-start(bf16[1,1,16,2048]{3,2,1,0:T(8,128)(2,1)} %copy.73) | copy-start | bytes 196612
  140.8 29.9 %copy-start.33 = (bf16[1,1,16,2048]{3,2,1,0:T(8,128)(2,1)S(1)}, bf16[1,1,16,2048]{3,2,1,0:T(8,128)(2,1)}, u32[]{:S(2)}) copy-start(bf16[1,1,16,2048]{3,2,1,0:T(8,128)(2,1)} %copy.74) | copy-start | bytes 196612
  141.4 75.4 %copy-start.40 = (s32[1,3]{1,0:T(1,128)S(1)}, s32[1,3]{1,0:T(1,128)}, u32[]{:S(2)}) copy-start(s32[1,3]{1,0:T(1,128)} %param.4) | copy-start | bytes 40
  211.5 28.8 %collective-permute-start.2 = (bf16[32,16,2048]{2,1,0:T(8,128)(2,1)S(1)}, bf16[32,16,2048]{2,1,0:T(8,128)(2,1)S(1)}, u32[]{:S(2)}, u32[]{:S(2)}) collective-permute-start(bf16[32,16,2048]{2,1,0:T(8,128)(2,1)S(1)} %bitcast.175), channel_id=1, source_target_pairs={{24,0},{32,8},{40,16},{48,24},{56,32},{64,40},{72,48},{80,56},{88,... | collective-permute-start | bytes 6291464 | tf_op jit(solution)/shard_map/ppermute | solution.py:16
  212.8 91.2 %collective-permute-start.1 = (bf16[32,16,2048]{2,1,0:T(8,128)(2,1)S(1)}, bf16[32,16,2048]{2,1,0:T(8,128)(2,1)S(1)}, u32[]{:S(2)}, u32[]{:S(2)}) collective-permute-start(bf16[32,16,2048]{2,1,0:T(8,128)(2,1)S(1)} %bitcast.176), channel_id=1, source_target_pairs={{16,0},{24,8},{32,16},{40,24},{48,32},{56,40},{64,48},{72,56},{80,... | collective-permute-start | bytes 6291464 | tf_op jit(solution)/shard_map/ppermute | solution.py:16
  214.1 91.9 %collective-permute-start = (bf16[32,16,2048]{2,1,0:T(8,128)(2,1)S(1)}, bf16[32,16,2048]{2,1,0:T(8,128)(2,1)S(1)}, u32[]{:S(2)}, u32[]{:S(2)}) collective-permute-start(bf16[32,16,2048]{2,1,0:T(8,128)(2,1)S(1)} %bitcast.177), channel_id=1, source_target_pairs={{8,0},{16,8},{24,16},{32,24},{40,32},{48,40},{56,48},{64,56},{72,6... | collective-permute-start | bytes 6291464 | tf_op jit(solution)/shard_map/ppermute | solution.py:16
  610.9 76.5 %collective-permute-start.5 = (bf16[32,16,2048]{2,1,0:T(8,128)(2,1)S(1)}, bf16[32,16,2048]{2,1,0:T(8,128)(2,1)}, u32[]{:S(2)}, u32[]{:S(2)}) collective-permute-start(bf16[32,16,2048]{2,1,0:T(8,128)(2,1)S(1)} %pad_maximum_fusion.5), channel_id=1, source_target_pairs={{0,24},{8,32},{16,40},{24,48},{32,56},{40,64},{48,72},{56,80},{64,... | collective-permute-start | bytes 6291464 | tf_op jit(solution)/shard_map/ppermute | solution.py:16
  617.7 87.3 %collective-permute-start.4 = (bf16[32,16,2048]{2,1,0:T(8,128)(2,1)S(1)}, bf16[32,16,2048]{2,1,0:T(8,128)(2,1)}, u32[]{:S(2)}, u32[]{:S(2)}) collective-permute-start(bf16[32,16,2048]{2,1,0:T(8,128)(2,1)S(1)} %pad_maximum_fusion.4), channel_id=1, source_target_pairs={{0,16},{8,24},{16,32},{24,40},{32,48},{40,56},{48,64},{56,72},{64,... | collective-permute-start | bytes 6291464 | tf_op jit(solution)/shard_map/ppermute | solution.py:16
  622.1 105.4 %collective-permute-start.3 = (bf16[32,16,2048]{2,1,0:T(8,128)(2,1)}, bf16[32,16,2048]{2,1,0:T(8,128)(2,1)}, u32[]{:S(2)}, u32[]{:S(2)}) collective-permute-start(bf16[32,16,2048]{2,1,0:T(8,128)(2,1)} %pad_maximum_fusion.3), channel_id=1, source_target_pairs={{0,8},{8,16},{16,24},{24,32},{32,40},{40,48},{48,56},{56,64},{64,7... | collective-permute-start | bytes 6291464 | tf_op jit(solution)/shard_map/ppermute | solution.py:16
  624.1 20.6 %copy-start.7 = (f32[32,16,1024]{2,1,0:T(8,128)S(1)}, f32[32,16,1024]{2,1,0:T(8,128)}, u32[]{:S(2)}) copy-start(f32[32,16,1024]{2,1,0:T(8,128)} %get-tuple-element.100) | copy-start | bytes 6291460
  624.1 20.6 %copy-start.8 = (f32[32,16,1024]{2,1,0:T(8,128)S(1)}, f32[32,16,1024]{2,1,0:T(8,128)}, u32[]{:S(2)}) copy-start(f32[32,16,1024]{2,1,0:T(8,128)} %get-tuple-element.101) | copy-start | bytes 6291460
  644.7 20.6 %copy-start.18 = (bf16[16,16,2048]{2,1,0:T(8,128)(2,1)S(1)}, bf16[16,16,2048]{2,1,0:T(8,128)(2,1)}, u32[]{:S(2)}) copy-start(bf16[16,16,2048]{2,1,0:T(8,128)(2,1)} %get-tuple-element.42) | copy-start | bytes 3145732
  733.3 36.5 %all-to-all-start.1 = ((bf16[32,16,2048]{2,1,0:T(8,128)(2,1)}), bf16[32,16,2048]{2,1,0:T(8,128)(2,1)S(1)}, u32[]{:S(2)}, u32[]{:S(2)}) async-start(bf16[32,16,2048]{2,1,0:T(8,128)(2,1)} %fusion.25), calls=%async_computation.1 | async-start | bytes 4194304 | tf_op jit(solution)/shard_map/all_to_all | solution.py:144
  823.2 18.2 %copy-start.42 = (s32[512]{0:T(512)S(1)}, s32[512]{0:T(512)}, u32[]{:S(2)}) copy-start(s32[512]{0:T(512)} %copy-done.41) | copy-start | bytes 6148
  823.2 18.2 %copy-start.44 = (pred[512]{0:T(512)(128)(4,1)S(1)}, pred[512]{0:T(512)(128)(4,1)}, u32[]{:S(2)}) copy-start(pred[512]{0:T(512)(128)(4,1)} %copy-done.43) | copy-start | bytes 1540
  841.4 19.0 %copy-start.1 = (bf16[1,512,2048]{2,1,0:T(8,128)(2,1)S(1)}, bf16[1,512,2048]{2,1,0:T(8,128)(2,1)}, u32[]{:S(2)}) copy-start(bf16[1,512,2048]{2,1,0:T(8,128)(2,1)} %param.3) | copy-start | bytes 6291460
  (21 other events, 103.8 us)
Sparse Core Ops, SparseCore 0:
  356.0 171.4 all-reduce.3
